TPU v7x, 256 devices: a whole 4x4x8 slice. The times are simulated.
256 devices in a mesh: grp: 4 (over y_hi, core), fsdp: 64 (over y_lo, x, z).
Axes of the slice: x: 4, y: 4 (y_hi: 2, y_lo: 2; y = y_hi * 2 + y_lo), z: 8, core: 2. Of those that a mesh axis runs over, the one named last changes fastest.
Arguments:
- traj_hidden: bfloat16 [262144, 4096], P(('grp', 'fsdp')), may hold values from -24 to 24
- traj_tokens: int32 [262144], P(('grp', 'fsdp')), may hold values from 0 to 511
- traj_action: int32 [262144], P(('grp', 'fsdp')), may hold values from 0 to 511
- traj_return: float32 [262144], P(('grp', 'fsdp')), may hold values from -6 to 6
- traj_episode: int32 [256, 1024], P(('grp', 'fsdp')), may hold values from 0 to 7, never falling along the last dimension, each value on 1 to 512 neighbouring positions
- roll_hidden: bfloat16 [16384, 4096], P(('grp', 'fsdp')), may hold values from -6 to 6
- roll_tokens: int32 [16384], P(('grp', 'fsdp')), may hold values from 0 to 511
- roll_action: int32 [16384], P(('grp', 'fsdp')), may hold values from 0 to 511
- station_table: bfloat16 [512, 4096], replicated, may hold values from -3 to 3
- norm_gain: float32 [4096], replicated, may hold values from 0.7 to 3.9
- head_weight: bfloat16 [4096, 512], P('fsdp'), may hold values from -6 to 6
Outputs:
- new_head: bfloat16 [4096, 512], P('fsdp')
- action_logp: float32 [16384], P(('grp', 'fsdp'))
- episode_logp: float32 [256], P(('grp', 'fsdp'))
Inputs may be any that keep to these rules, and one draw needn't show every extreme that they name: `traj_episode`: within each block of 1024 tokens the episode numbers never fall and every number 0 to 7 occurs.
All inputs are finite; a program needn't handle non-finite values.
Results may differ from a plain program's by a relative error of at most 0.0034.
Values may be sent and summed in bfloat16 or wider, within the bound.
A program may use at most 64 MiB of HBM per device.

v0:
```python
import jax
import jax.numpy as jnp
from jax import lax
from jax.sharding import PartitionSpec as P

ACTIONS = 512
STATIONS = 512
EPI_BLK = 8
STEPS = 64
step_length = 8.0


def station_rows(hidden, tokens, table, gain):
    lookup = (tokens[:, None] == jnp.arange(STATIONS, dtype=jnp.int32)[None, :]).astype(
        jnp.bfloat16
    )
    embedded = jnp.dot(lookup, table, preferred_element_type=jnp.float32)
    mixed = hidden.astype(jnp.float32) + embedded
    power = jnp.mean(mixed * mixed, axis=-1, keepdims=True)
    return (mixed * lax.rsqrt(power + 1e-05) * gain).astype(jnp.bfloat16)


def add_columns(left, piece):
    return jnp.dot(left, piece, preferred_element_type=jnp.float32)


def picked_logp(logits, actions):
    top = jnp.max(logits, axis=-1, keepdims=True)
    total = jnp.log(jnp.sum(jnp.exp(logits - top), axis=-1)) + top[:, 0]
    chosen = (actions[:, None] == jnp.arange(ACTIONS, dtype=jnp.int32)[None, :]).astype(jnp.float32)
    return jnp.sum(logits * chosen, axis=-1) - total


def episode_advantage(returns, episode):
    member = (episode[:, None] == jnp.arange(EPI_BLK, dtype=jnp.int32)[None, :]).astype(jnp.float32)
    sums = jnp.dot(member.T, returns, precision=lax.Precision.HIGHEST)
    counts = jnp.sum(member, axis=0)
    baseline = jnp.dot(member, sums / counts, precision=lax.Precision.HIGHEST)
    return returns - baseline


def outer_rows(left, right):
    return lax.dot_general(
        left, right, (((0,), (0,)), ((), ())), preferred_element_type=jnp.float32
    )


def local(
    traj_hidden,
    traj_tokens,
    traj_action,
    traj_return,
    traj_episode,
    roll_hidden,
    roll_tokens,
    roll_action,
    station_table,
    norm_gain,
    head_weight,
):
    features = station_rows(traj_hidden, traj_tokens, station_table, norm_gain)
    rollout = station_rows(roll_hidden, roll_tokens, station_table, norm_gain)
    advantage = episode_advantage(traj_return, traj_episode[0])
    logits = add_columns(features, lax.all_gather(head_weight, "fsdp", axis=0, tiled=True))
    top = jnp.max(logits, axis=-1, keepdims=True)
    expo = jnp.exp(logits - top)
    probs = expo / jnp.sum(expo, axis=-1, keepdims=True)
    chosen = (traj_action[:, None] == jnp.arange(ACTIONS, dtype=jnp.int32)[None, :]).astype(
        jnp.float32
    )
    scores = (advantage[:, None] * (probs - chosen)).astype(jnp.bfloat16)
    gathered, all_scores = (features, scores)
    grad_shard = lax.psum_scatter(
        outer_rows(gathered, all_scores), "fsdp", scatter_dimension=0, tiled=True
    )
    grad_shard = lax.psum(grad_shard, "grp")
    squares = lax.psum(jnp.sum(grad_shard * grad_shard), "fsdp")
    gnorm = jnp.sqrt(squares + 1e-06)
    new_head = (head_weight.astype(jnp.float32) - step_length * grad_shard / gnorm).astype(
        jnp.bfloat16
    )
    roll_logits = add_columns(rollout, lax.all_gather(new_head, "fsdp", axis=0, tiled=True))
    action_logp = picked_logp(roll_logits, roll_action)
    episode_logp = jnp.sum(action_logp.reshape(-1, STEPS), axis=1)
    return (new_head, action_logp, episode_logp)


def solution(mesh):
    placed = (
        P(("grp", "fsdp"), None),
        P(("grp", "fsdp")),
        P(("grp", "fsdp")),
        P(("grp", "fsdp")),
        P(("grp", "fsdp"), None),
        P(("grp", "fsdp"), None),
        P(("grp", "fsdp")),
        P(("grp", "fsdp")),
        P(),
        P(),
        P("fsdp", None),
    )
    return jax.shard_map(
        local,
        mesh=mesh,
        in_specs=placed,
        out_specs=(P("fsdp", None), P(("grp", "fsdp")), P(("grp", "fsdp"))),
        check_vma=False,
    )
```

profile of v0, /device:TPU:16, one launch (start us, length us, event | category | flops | bytes accessed | tf_op | source)
XLA Modules:
  0.0 1174.0 jit_solution(12649572377093902791)
XLA Ops:
  7.2 0.0 all-gather.3.cloned.1.call-start
  7.2 0.7 all-gather.3.cloned.1.call-update
  7.9 0.0 reduce-scatter.2.cloned.1.call-start
  7.9 0.8 convert_reduce_fusion
  8.8 0.8 fusion.3
  9.6 0.9 fusion.14
  10.4 0.7 sub.30
  11.1 0.0 copy-start.3
  11.1 8.8 multiply_reduce_fusion
  19.9 0.0 copy-done.3
  20.0 8.9 multiply_convert_fusion
  28.8 0.0 copy-start.6
  28.8 287.5 %all-gather.3.cloned.1.call-done = bf16[4096,512]{1,0:T(8,128)(2,1)} async-done(((bf16[64,512]{1,0:T(8,128)(2,1)}), bf16[4096,512]{1,0:T(8,128)(2,1)}) %all-gather.3.cloned.1.call-update) | async-done | bytes 4194320 | tf_op jit(solution)/shard_map/all_gather | solution.py:64
  316.3 0.0 copy-start
  316.3 8.4 fusion.18
  324.7 0.3 fusion.1
  325.1 0.0 copy-done.6
  325.1 0.0 copy-done
  325.1 7.7 fusion.4
  332.7 0.0 copy-start.2
  332.8 0.0 copy-start.1
  332.8 0.0 copy-start.4
  332.8 0.0 reduce-scatter.2.cloned.1.call-update
  332.8 0.0 all-reduce.2.cloned.1.call-start
  332.8 329.6 %reduce-scatter.2.cloned.1.call-done = f32[64,512]{1,0:T(8,128)} async-done(((f32[4096,512]{1,0:T(8,128)}), f32[64,512]{1,0:T(8,128)}) %reduce-scatter.2.cloned.1.call-update) | async-done | bytes 131088 | tf_op jit(solution)/shard_map/reduce_scatter | solution.py:73
  662.4 0.0 all-reduce.2.cloned.1.call-update
  662.5 0.0 all-gather.5.cloned.1.call-start
  662.5 39.2 %all-reduce.2.cloned.1.call-done = f32[64,512]{1,0:T(8,128)} async-done(((f32[64,512]{1,0:T(8,128)}), f32[64,512]{1,0:T(8,128)}) %all-reduce.2.cloned.1.call-update) | async-done | bytes 131088 | tf_op jit(solution)/shard_map/psum | solution.py:76
  701.7 1.5 multiply_reduce_fusion.2
  703.3 159.9 %psum.15 = f32[]{:T(128)} all-reduce(f32[]{:T(128)} %multiply_reduce_fusion.2), channel_id=1, replica_groups=mesh['grp'=4,'fsdp'=64] {'fsdp'}, use_global_device_ids=true, to_apply=%region_7.0 | all-reduce | flops 1 | bytes 8 | tf_op jit(solution)/shard_map/psum | solution.py:77
  863.8 0.0 copy-done.2
  863.8 1.6 subtract_convert_fusion
  865.4 0.0 all-gather.5.cloned.1.call-update
  865.4 0.0 copy-done.1
  865.4 0.0 copy-done.4
  865.4 0.0 copy-start.5
  865.4 3.2 multiply_reduce_fusion.1
  868.7 294.3 %all-gather.5.cloned.1.call-done = bf16[4096,512]{1,0:T(8,128)(2,1)} async-done(((bf16[64,512]{1,0:T(8,128)(2,1)}), bf16[4096,512]{1,0:T(8,128)(2,1)}) %all-gather.5.cloned.1.call-update) | async-done | bytes 4194320 | tf_op jit(solution)/shard_map/all_gather | solution.py:82
  1163.0 3.2 fusion.19
  1166.2 0.0 copy-done.5
  1166.2 0.2 exponential_reduce_fusion
  1166.4 1.1 fusion.17
  (2 shorter events, 0.0 us)
Async XLA Ops:
  7.2 309.2 %all-gather.3.cloned.1.call-start = ((), (), s32[]{:S(2)}) async-start(), calls=%async_computation.1 | async-start | bytes 4259840 | tf_op jit(solution)/shard_map/all_gather | solution.py:64
  7.9 654.5 %reduce-scatter.2.cloned.1.call-start = ((), (), s32[]{:S(2)}) async-start(), calls=%async_computation.2 | async-start | bytes 8519680 | tf_op jit(solution)/shard_map/reduce_scatter | solution.py:73
  11.1 8.8 copy-start.3
  28.8 296.3 %copy-start.6 = (s32[1024]{0:T(1024)S(1)}, s32[1024]{0:T(1024)}, u32[]{:S(2)}) copy-start(s32[1024]{0:T(1024)} %param.13) | copy-start | bytes 12292
  316.3 8.8 copy-start
  332.7 531.1 %copy-start.2 = (bf16[64,512]{1,0:T(8,128)(2,1)S(1)}, bf16[64,512]{1,0:T(8,128)(2,1)}, u32[]{:S(2)}) copy-start(bf16[64,512]{1,0:T(8,128)(2,1)} %param.21) | copy-start | bytes 196612
  332.8 532.7 %copy-start.1 = (bf16[64,4096]{1,0:T(8,128)(2,1)S(1)}, bf16[64,4096]{1,0:T(8,128)(2,1)}, u32[]{:S(2)}) copy-start(bf16[64,4096]{1,0:T(8,128)(2,1)} %param.16) | copy-start | bytes 1572868
  332.8 532.7 %copy-start.4 = (s32[64]{0:T(128)S(1)}, s32[64]{0:T(128)}, u32[]{:S(2)}) copy-start(s32[64]{0:T(128)} %param.17) | copy-start | bytes 772
  332.8 369.0 %all-reduce.2.cloned.1.call-start = ((), (), s32[]{:S(2)}) async-start(), calls=%async_computation.3 | async-start | bytes 262144 | tf_op jit(solution)/shard_map/psum | solution.py:76
  662.5 500.5 %all-gather.5.cloned.1.call-start = ((), (), s32[]{:S(2)}) async-start(), calls=%async_computation.4 | async-start | bytes 4259840 | tf_op jit(solution)/shard_map/all_gather | solution.py:82
  865.4 300.7 %copy-start.5 = (s32[64]{0:T(128)S(1)}, s32[64]{0:T(128)}, u32[]{:S(2)}) copy-start(s32[64]{0:T(128)} %param.18) | copy-start | bytes 772
Sparse Core Ops, SparseCore 0:
  9.8 306.4 all-gather.2
  332.9 329.4 reduce-scatter.1
  665.1 36.6 all-reduce.1
  865.5 297.4 all-gather.4
where the time goes:
time: 1170 us
  waiting for transfers between devices  951 us (81%)
  blocking collectives  160 us (14%)
  matrix products  32.9 us (3%)
  other arithmetic  15.1 us (1%)
  between operations  14.6 us (1%)
    reduce_scatter x1, waiting for transfers between devices, local(): lax.psum_scatter(outer_rows(gathered, all_scores), 'fsdp', scatter_dimens...  330 us
    all_gather x1, waiting for transfers between devices, local(): lax.all_gather(new_head, 'fsdp', axis=0, tiled=True)  294 us
    all_gather x1, waiting for transfers between devices, local(): lax.all_gather(head_weight, 'fsdp', axis=0, tiled=True)  288 us
    psum x1, blocking collectives, local(): squares = lax.psum(jnp.sum(grad_shard * grad_shard), 'fsdp')  160 us
    psum x1, waiting for transfers between devices, local(): grad_shard = lax.psum(grad_shard, 'grp')  39.2 us
  transfers between devices with their start and end apart: 4, of which 4 were waited for; matrix products, arithmetic and copies ran while one was open for 2% of the time, Pallas kernels for 0%

commit v1 on v0

--- a/solution.py
+++ b/solution.py
@@ -73,7 +73,8 @@
     grad_shard = lax.psum_scatter(
         outer_rows(gathered, all_scores), "fsdp", scatter_dimension=0, tiled=True
     )
-    grad_shard = lax.psum(grad_shard, "grp")
+    blocks = lax.all_gather(grad_shard, "grp")
+    grad_shard = jnp.sum(blocks, axis=0)
     squares = lax.psum(jnp.sum(grad_shard * grad_shard), "fsdp")
     gnorm = jnp.sqrt(squares + 1e-06)
     new_head = (head_weight.astype(jnp.float32) - step_length * grad_shard / gnorm).astype(

time: 1170 us -> 1140 us (0.974)
  waiting for transfers between devices: 951 us -> 912 us
    psum x1 -> x0, waiting for transfers between devices: 39.2 us -> none  [local(): grad_shard = lax.psum(grad_shard, 'grp')]
  transfers between devices with their start and end apart: 4 -> 3, of which waited for: 4 -> 3; matrix products, arithmetic and copies ran while one was open for 2% -> 2% of each run, Pallas kernels for 0% -> 0%
where the time goes in v1:
time: 1140 us
  waiting for transfers between devices  912 us (80%)
  blocking collectives  163 us (14%)
  matrix products  32.9 us (3%)
  between operations  14.5 us (1%)
  other arithmetic  13.4 us (1%)
    reduce_scatter x1, waiting for transfers between devices, local(): lax.psum_scatter(outer_rows(gathered, all_scores), 'fsdp', scatter_dimens...  330 us
    all_gather x1, waiting for transfers between devices, local(): lax.all_gather(new_head, 'fsdp', axis=0, tiled=True)  294 us
    all_gather x1, waiting for transfers between devices, local(): lax.all_gather(head_weight, 'fsdp', axis=0, tiled=True)  288 us
    psum x1, blocking collectives, local(): squares = lax.psum(jnp.sum(grad_shard * grad_shard), 'fsdp')  155 us
  transfers between devices with their start and end apart: 3, of which 3 were waited for; matrix products, arithmetic and copies ran while one was open for 2% of the time, Pallas kernels for 0%

profile of v1, /device:TPU:16, one launch (start us, length us, event | category | flops | bytes accessed | tf_op | source)
XLA Modules:
  0.0 1135.9 jit_solution(4385023929642320360)
XLA Ops:
  7.2 0.0 all-gather.4.cloned.1.call-start
  7.2 0.7 all-gather.4.cloned.1.call-update
  7.9 0.0 reduce-scatter.2.cloned.1.call-start
  7.9 0.8 convert_reduce_fusion
  8.8 0.8 fusion.3
  9.6 0.9 fusion.14
  10.4 0.7 sub.30
  11.1 0.0 copy-start.3
  11.1 8.8 multiply_reduce_fusion
  19.9 0.0 copy-done.3
  20.0 8.9 multiply_convert_fusion
  28.8 0.0 copy-start.6
  28.8 287.5 %all-gather.4.cloned.1.call-done = bf16[4096,512]{1,0:T(8,128)(2,1)} async-done(((bf16[64,512]{1,0:T(8,128)(2,1)}), bf16[4096,512]{1,0:T(8,128)(2,1)}) %all-gather.4.cloned.1.call-update) | async-done | bytes 4194320 | tf_op jit(solution)/shard_map/all_gather | solution.py:64
  316.3 0.0 copy-start
  316.3 8.4 fusion.18
  324.7 0.3 fusion.1
  325.1 0.0 copy-done.6
  325.1 0.0 copy-done
  325.1 7.7 fusion.4
  332.7 0.0 copy-start.2
  332.8 0.0 copy-start.1
  332.8 0.0 copy-start.4
  332.8 0.0 reduce-scatter.2.cloned.1.call-update
  332.8 0.0 all-gather.6.cloned.1.call-start
  332.8 329.6 %reduce-scatter.2.cloned.1.call-done = f32[64,512]{1,0:T(8,128)} async-done(((f32[4096,512]{1,0:T(8,128)}), f32[64,512]{1,0:T(8,128)}) %reduce-scatter.2.cloned.1.call-update) | async-done | bytes 131088 | tf_op jit(solution)/shard_map/reduce_scatter | solution.py:73
  662.4 8.2 all-gather
  670.7 0.6 multiply_reduce_fusion.2
  671.3 154.5 %psum.7 = f32[]{:T(128)} all-reduce(f32[]{:T(128)} %multiply_reduce_fusion.2), channel_id=1, replica_groups=mesh['grp'=4,'fsdp'=64] {'fsdp'}, use_global_device_ids=true, to_apply=%region_7.0 | all-reduce | flops 1 | bytes 8 | tf_op jit(solution)/shard_map/psum | solution.py:78
  826.5 0.0 copy-done.2
  826.5 0.7 subtract_convert_fusion
  827.2 0.0 all-gather.6.cloned.1.call-update
  827.2 0.0 copy-done.1
  827.2 0.0 copy-done.4
  827.2 0.0 copy-start.5
  827.3 3.2 multiply_reduce_fusion.1
  830.5 294.3 %all-gather.6.cloned.1.call-done = bf16[4096,512]{1,0:T(8,128)(2,1)} async-done(((bf16[64,512]{1,0:T(8,128)(2,1)}), bf16[4096,512]{1,0:T(8,128)(2,1)}) %all-gather.6.cloned.1.call-update) | async-done | bytes 4194320 | tf_op jit(solution)/shard_map/all_gather | solution.py:83
  1124.8 3.2 fusion.19
  1128.0 0.0 copy-done.5
  1128.0 0.2 exponential_reduce_fusion
  1128.2 1.1 fusion.17
  (3 shorter events, 0.0 us)
Async XLA Ops:
  7.2 309.2 %all-gather.4.cloned.1.call-start = ((), (), s32[]{:S(2)}) async-start(), calls=%async_computation.1 | async-start | bytes 4259840 | tf_op jit(solution)/shard_map/all_gather | solution.py:64
  7.9 654.5 %reduce-scatter.2.cloned.1.call-start = ((), (), s32[]{:S(2)}) async-start(), calls=%async_computation.2 | async-start | bytes 8519680 | tf_op jit(solution)/shard_map/reduce_scatter | solution.py:73
  11.1 8.8 copy-start.3
  28.8 296.3 %copy-start.6 = (s32[1024]{0:T(1024)S(1)}, s32[1024]{0:T(1024)}, u32[]{:S(2)}) copy-start(s32[1024]{0:T(1024)} %param.13) | copy-start | bytes 12292
  316.3 8.8 copy-start
  332.7 493.8 %copy-start.2 = (bf16[64,512]{1,0:T(8,128)(2,1)S(1)}, bf16[64,512]{1,0:T(8,128)(2,1)}, u32[]{:S(2)}) copy-start(bf16[64,512]{1,0:T(8,128)(2,1)} %param.21) | copy-start | bytes 196612
  332.8 494.5 %copy-start.1 = (bf16[64,4096]{1,0:T(8,128)(2,1)S(1)}, bf16[64,4096]{1,0:T(8,128)(2,1)}, u32[]{:S(2)}) copy-start(bf16[64,4096]{1,0:T(8,128)(2,1)} %param.16) | copy-start | bytes 1572868
  332.8 494.5 %copy-start.4 = (s32[64]{0:T(128)S(1)}, s32[64]{0:T(128)}, u32[]{:S(2)}) copy-start(s32[64]{0:T(128)} %param.17) | copy-start | bytes 772
  332.8 792.0 %all-gather.6.cloned.1.call-start = ((), (), s32[]{:S(2)}) async-start(), calls=%async_computation.3 | async-start | bytes 4259840 | tf_op jit(solution)/shard_map/all_gather | solution.py:83
  827.2 300.7 %copy-start.5 = (s32[64]{0:T(128)S(1)}, s32[64]{0:T(128)}, u32[]{:S(2)}) copy-start(s32[64]{0:T(128)} %param.18) | copy-start | bytes 772
Sparse Core Ops, SparseCore 0:
  9.8 306.4 all-gather.3
  332.9 329.4 reduce-scatter.1
  827.3 297.4 all-gather.5

commit v2 on v0

--- a/solution.py
+++ b/solution.py
@@ -79,7 +79,14 @@
     new_head = (head_weight.astype(jnp.float32) - step_length * grad_shard / gnorm).astype(
         jnp.bfloat16
     )
-    roll_logits = add_columns(rollout, lax.all_gather(new_head, "fsdp", axis=0, tiled=True))
+
+    def play_sources_all(xin, row_axis, dim_no):
+        shaped = tuple((xin for _ in range(lax.axis_size(row_axis))))
+        fresh = lax.all_to_all(jnp.stack(shaped, axis=0), row_axis, 0, 0)
+        o_now = jnp.concatenate(fresh, axis=dim_no)
+        return o_now
+
+    roll_logits = add_columns(rollout, play_sources_all(new_head, "fsdp", 0))
     action_logp = picked_logp(roll_logits, roll_action)
     episode_logp = jnp.sum(action_logp.reshape(-1, STEPS), axis=1)
     return (new_head, action_logp, episode_logp)

time: 1170 us -> 955 us (0.82)
  waiting for transfers between devices: 951 us -> 721 us
    all_gather x1 -> x0, waiting for transfers between devices: 294 us -> none  [local(): lax.all_gather(new_head, 'fsdp', axis=0, tiled=True)]
    all_to_all x0 -> x1, waiting for transfers between devices: none -> 63.7 us  [play_sources_all(): fresh = lax.all_to_all(jnp.stack(shaped, axis=0), row_axis, 0, 0)]
  transfers between devices with their start and end apart: 4 -> 4, of which waited for: 4 -> 4; matrix products, arithmetic and copies ran while one was open for 2% -> 3% of each run, Pallas kernels for 0% -> 0%
where the time goes in v2:
time: 955 us; the launch traced here: 952 us
  waiting for transfers between devices  721 us (75%)
  blocking collectives  161 us (17%)
  matrix products  32.9 us (3%)
  between operations  14.6 us (2%)
  other arithmetic  14.5 us (2%)
    reduce_scatter x1, waiting for transfers between devices, local(): lax.psum_scatter(outer_rows(gathered, all_scores), 'fsdp', scatter_dimens...  330 us
    all_gather x1, waiting for transfers between devices, local(): lax.all_gather(head_weight, 'fsdp', axis=0, tiled=True)  288 us
    psum x1, blocking collectives, local(): squares = lax.psum(jnp.sum(grad_shard * grad_shard), 'fsdp')  161 us
    all_to_all x1, waiting for transfers between devices, play_sources_all(): fresh = lax.all_to_all(jnp.stack(shaped, axis=0), row_axis, 0, 0)  63.7 us
    psum x1, waiting for transfers between devices, local(): grad_shard = lax.psum(grad_shard, 'grp')  39.4 us
  transfers between devices with their start and end apart: 4, of which 4 were waited for; matrix products, arithmetic and copies ran while one was open for 3% of the time, Pallas kernels for 0%

profile of v2, /device:TPU:16, one launch (start us, length us, event | category | flops | bytes accessed | tf_op | source)
XLA Modules:
  0.0 952.3 jit_solution(6792862771197155516)
XLA Ops:
  7.2 0.0 all-gather.2.cloned.1.call-start
  7.2 0.7 all-gather.2.cloned.1.call-update
  7.9 0.0 reduce-scatter.2.cloned.1.call-start
  7.9 0.8 convert_reduce_fusion
  8.8 0.8 fusion.3
  9.6 0.9 fusion.14
  10.4 0.7 sub.30
  11.1 0.0 copy-start.4
  11.1 8.8 multiply_reduce_fusion
  19.9 0.0 copy-done.4
  20.0 8.9 multiply_convert_fusion
  28.8 0.0 copy-start.7
  28.8 287.5 %all-gather.2.cloned.1.call-done = bf16[4096,512]{1,0:T(8,128)(2,1)} async-done(((bf16[64,512]{1,0:T(8,128)(2,1)}), bf16[4096,512]{1,0:T(8,128)(2,1)}) %all-gather.2.cloned.1.call-update) | async-done | bytes 4194320 | tf_op jit(solution)/shard_map/all_gather | solution.py:64
  316.3 0.0 copy-start
  316.3 8.4 fusion.18
  324.7 0.3 fusion.1
  325.1 0.0 copy-done.7
  325.1 0.0 copy-done
  325.1 7.7 fusion.4
  332.7 0.0 copy-start.3
  332.8 0.0 reduce-scatter.2.cloned.1.call-update
  332.8 0.0 all-reduce.2.cloned.1.call-start
  332.8 329.6 %reduce-scatter.2.cloned.1.call-done = f32[64,512]{1,0:T(8,128)} async-done(((f32[4096,512]{1,0:T(8,128)}), f32[64,512]{1,0:T(8,128)}) %reduce-scatter.2.cloned.1.call-update) | async-done | bytes 131088 | tf_op jit(solution)/shard_map/reduce_scatter | solution.py:73
  662.4 0.0 all-reduce.2.cloned.1.call-update
  662.5 39.4 %all-reduce.2.cloned.1.call-done = f32[64,512]{1,0:T(8,128)} async-done(((f32[64,512]{1,0:T(8,128)}), f32[64,512]{1,0:T(8,128)}) %all-reduce.2.cloned.1.call-update) | async-done | bytes 131088 | tf_op jit(solution)/shard_map/psum | solution.py:76
  701.8 1.5 multiply_reduce_fusion.2
  703.4 161.0 %psum.15 = f32[]{:T(128)} all-reduce(f32[]{:T(128)} %multiply_reduce_fusion.2), channel_id=1, replica_groups=mesh['grp'=4,'fsdp'=64] {'fsdp'}, use_global_device_ids=true, to_apply=%region_7.0 | all-reduce | flops 1 | bytes 8 | tf_op jit(solution)/shard_map/psum | solution.py:77
  865.1 0.0 copy-done.3
  865.1 0.9 subtract_convert_fusion
  866.0 0.0 copy-start.2
  866.0 2.5 stack.2
  868.5 0.0 copy-start.1
  868.5 0.0 copy-start.5
  868.5 0.0 copy-done.2
  868.5 5.8 all-to-all-start
  874.3 0.0 copy-done.1
  874.3 0.0 copy-done.5
  874.3 0.0 copy-start.6
  874.3 3.2 multiply_reduce_fusion.1
  877.6 63.7 %all-to-all-done = bf16[64,64,512]{2,1,0:T(8,128)(2,1)} async-done(((bf16[64,64,512]{2,1,0:T(8,128)(2,1)}), bf16[64,64,512]{2,1,0:T(8,128)(2,1)}, u32[]{:S(2)}, u32[]{:S(2)}) %all-to-all-start) | async-done | bytes 4194336 | tf_op jit(solution)/shard_map/all_to_all | solution.py:85
  941.2 3.2 fusion.19
  944.4 0.0 copy-done.6
  944.4 0.2 exponential_reduce_fusion
  944.6 1.1 fusion.17
  (2 shorter events, 0.0 us)
Async XLA Ops:
  7.2 309.2 %all-gather.2.cloned.1.call-start = ((), (), s32[]{:S(2)}) async-start(), calls=%async_computation.2 | async-start | bytes 4259840 | tf_op jit(solution)/shard_map/all_gather | solution.py:64
  7.9 654.5 %reduce-scatter.2.cloned.1.call-start = ((), (), s32[]{:S(2)}) async-start(), calls=%async_computation.3 | async-start | bytes 8519680 | tf_op jit(solution)/shard_map/reduce_scatter | solution.py:73
  11.1 8.8 copy-start.4
  28.8 296.3 %copy-start.7 = (s32[1024]{0:T(1024)S(1)}, s32[1024]{0:T(1024)}, u32[]{:S(2)}) copy-start(s32[1024]{0:T(1024)} %param.13) | copy-start | bytes 12292
  316.3 8.8 copy-start
  332.7 532.3 %copy-start.3 = (bf16[64,512]{1,0:T(8,128)(2,1)S(1)}, bf16[64,512]{1,0:T(8,128)(2,1)}, u32[]{:S(2)}) copy-start(bf16[64,512]{1,0:T(8,128)(2,1)} %param.21) | copy-start | bytes 196612
  332.8 369.1 %all-reduce.2.cloned.1.call-start = ((), (), s32[]{:S(2)}) async-start(), calls=%async_computation.4 | async-start | bytes 262144 | tf_op jit(solution)/shard_map/psum | solution.py:76
  866.0 2.5 copy-start.2
  868.5 5.8 copy-start.1
  868.5 5.8 copy-start.5
  868.5 72.7 %all-to-all-start = ((bf16[64,64,512]{2,1,0:T(8,128)(2,1)}), bf16[64,64,512]{2,1,0:T(8,128)(2,1)}, u32[]{:S(2)}, u32[]{:S(2)}) async-start(bf16[64,64,512]{2,1,0:T(8,128)(2,1)} %stack.2), calls=%async_computation.1 | async-start | bytes 8388608 | tf_op jit(solution)/shard_map/all_to_all | solution.py:85
  874.3 70.1 %copy-start.6 = (s32[64]{0:T(128)S(1)}, s32[64]{0:T(128)}, u32[]{:S(2)}) copy-start(s32[64]{0:T(128)} %param.18) | copy-start | bytes 772
Sparse Core Ops, SparseCore 0:
  9.8 306.4 all-gather.1
  332.9 329.4 reduce-scatter.1
  665.1 36.7 all-reduce.1
